TPU v7x, 32 devices: a whole 2x2x4 slice. The times are simulated.
32 devices in a mesh: section: 2 (over y), design: 8 (over z, x), batch: 2 (over core).
Axes of the slice: x: 2, y: 2, z: 4, core: 2. Of those that a mesh axis runs over, the one named last changes fastest.
Arguments:
- samples: float32 [64, 4096], replicated, may hold values from -6 to 6
- order: int32 [4096], P('batch'), may hold values from 0 to 4095, each once
- design_points: bfloat16 [2, 64, 16384], P('section', None, 'design'), may hold values from -6 to 6
- weights: bfloat16 [2, 64, 16384], P('section', None, 'design'), may hold values from -2 to 2
- length_sq: float32 [2, 64], replicated, may hold values from 8 to 128
Outputs:
- moments: float32 [2, 4, 64, 1024], P('section', None, None, ('batch', 'design'))
Inputs may be any that keep to these rules, and one draw needn't show every extreme that they name: `order`: each sample index appears exactly once.
All inputs are finite; a program needn't handle non-finite values.
Results may differ from a plain program's by a relative error of at most 0.0037.
Values may be sent and summed in bfloat16 or wider, within the bound.
A program may use at most 64 MiB of HBM per device.

v0:
```python
import jax
import jax.numpy as jnp
from jax import lax
from jax.sharding import PartitionSpec as P

MICRO = 512


def passed_along(block, axis, distance):
    devices = range(lax.axis_size(axis))
    route = [(i - distance, i) for i in devices if i - distance in devices]
    return lax.ppermute(block, axis, route)


def local_sum(mean_in, var_in, points, squares, weight_rows, lengths):
    denom = lengths[:, None] + 2.0 * var_in
    offset = jnp.sum(mean_in * mean_in / denom, axis=0)
    log_scale = -0.5 * jnp.sum(jnp.log(1.0 + 2.0 * var_in / lengths[:, None]), axis=0)
    scaled = (mean_in / denom).astype(jnp.bfloat16)
    inverse = (1.0 / denom).astype(jnp.bfloat16)
    cross = lax.dot_general(
        scaled, points, (((0,), (0,)), ((), ())), preferred_element_type=jnp.float32
    )
    quad = lax.dot_general(
        inverse, squares, (((0,), (0,)), ((), ())), preferred_element_type=jnp.float32
    )
    kernel = jnp.exp(log_scale[:, None] - offset[:, None] + 2.0 * cross - quad).astype(jnp.bfloat16)
    return lax.dot_general(
        weight_rows, kernel, (((1,), (1,)), ((), ())), preferred_element_type=jnp.float32
    )


def square_of(points):
    wide = points.astype(jnp.float32)
    return (wide * wide).astype(jnp.bfloat16)


def shards(samples, order, design_points, weights, length_sq):
    section_index = lax.axis_index("section")
    is_first = section_index == 0
    points = design_points[0]
    weight_rows = weights[0]
    lengths = jnp.where(is_first, length_sq[0], length_sq[1])
    squares = square_of(points)
    feat = points.shape[0]
    half = feat // 2
    count = order.shape[0] // MICRO
    share = MICRO // lax.axis_size("design")
    column = lax.axis_index("design") * share

    def pick(turn):
        indices = order[turn * MICRO : (turn + 1) * MICRO]
        return jnp.take(samples, indices, axis=1)

    received = jnp.zeros((feat, MICRO), jnp.float32)
    zeros_rest = jnp.zeros((feat - half, MICRO), jnp.float32)
    firsts = []
    seconds = []
    for turn in range(count + 1):
        current = pick(min(turn, count - 1))
        earlier = pick(max(turn - 1, 0))
        moments_in = received
        later_mean = jnp.concatenate([moments_in[:half], earlier[half:]], axis=0)
        later_var = jnp.concatenate([moments_in[half:], zeros_rest], axis=0)
        mean_in = jnp.where(is_first, current, later_mean)
        var_in = jnp.where(is_first, 0.0, later_var)
        partial_sum = local_sum(mean_in, var_in, points, squares, weight_rows, lengths)
        summed = lax.psum(partial_sum, "design")
        layer_out = jnp.where(
            is_first,
            jnp.concatenate([summed[:half], jax.nn.softplus(summed[half:])], axis=0),
            summed,
        )
        received = passed_along(layer_out, "section", 1)
        block = lax.dynamic_slice_in_dim(layer_out, column, share, 1)
        if turn < count:
            firsts.append(block)
        if turn > 0:
            seconds.append(block)
    result = jnp.where(is_first, jnp.stack(firsts, axis=0), jnp.stack(seconds, axis=0))
    return result[None]


def solution(mesh):
    placed = (P(), P("batch"), P("section", None, "design"), P("section", None, "design"), P())
    return jax.shard_map(
        shards,
        mesh=mesh,
        in_specs=placed,
        out_specs=P("section", None, None, ("batch", "design")),
        check_vma=False,
    )
```

profile of v0, /device:TPU:4, one launch (start us, length us, event | category | flops | bytes accessed | tf_op | source)
XLA Modules:
  0.0 446.3 jit_solution(6106497824247773900)
XLA Ops:
  9.5 1.8 copy.6
  12.6 2.7 fusion.23
  16.1 4.4 fusion.9
  20.5 71.8 %all-reduce.11.cloned.1.call-done = f32[64,512]{1,0:T(8,128)} async-done(((f32[64,512]{1,0:T(8,128)}), f32[64,512]{1,0:T(8,128)}) %all-reduce.11.cloned.1.call-update) | async-done | bytes 131088 | tf_op jit(solution)/shard_map/psum | solution.py:68
  94.2 1.3 collective-permute-start
  96.7 4.4 collective-permute-done
  101.2 2.7 fusion.21
  103.9 4.4 fusion.8
  108.4 69.7 %all-reduce.13.cloned.1.call-done = f32[64,512]{1,0:T(8,128)} async-done(((f32[64,512]{1,0:T(8,128)}), f32[64,512]{1,0:T(8,128)}) %all-reduce.13.cloned.1.call-update) | async-done | bytes 131088 | tf_op jit(solution)/shard_map/psum | solution.py:68
  179.9 1.3 collective-permute-start.1
  182.4 4.5 %collective-permute-done.1 = f32[64,512]{1,0:T(8,128)} collective-permute-done((f32[64,512]{1,0:T(8,128)S(1)}, f32[64,512]{1,0:T(8,128)}, u32[]{:S(2)}, u32[]{:S(2)}) %collective-permute-start.1) | collective-permute-done | bytes 131104 | tf_op jit(solution)/shard_map/ppermute | solution.py:12
  187.9 2.7 fusion.19
  190.6 4.4 fusion.7
  195.1 69.7 %all-reduce.15.cloned.1.call-done = f32[64,512]{1,0:T(8,128)} async-done(((f32[64,512]{1,0:T(8,128)}), f32[64,512]{1,0:T(8,128)}) %all-reduce.15.cloned.1.call-update) | async-done | bytes 131088 | tf_op jit(solution)/shard_map/psum | solution.py:68
  266.7 1.3 collective-permute-start.2
  269.1 4.5 %collective-permute-done.2 = f32[64,512]{1,0:T(8,128)} collective-permute-done((f32[64,512]{1,0:T(8,128)S(1)}, f32[64,512]{1,0:T(8,128)}, u32[]{:S(2)}, u32[]{:S(2)}) %collective-permute-start.2) | collective-permute-done | bytes 131104 | tf_op jit(solution)/shard_map/ppermute | solution.py:12
  274.6 2.7 fusion.17
  277.4 4.4 fusion.6
  281.9 69.7 %all-reduce.17.cloned.1.call-done = f32[64,512]{1,0:T(8,128)} async-done(((f32[64,512]{1,0:T(8,128)}), f32[64,512]{1,0:T(8,128)}) %all-reduce.17.cloned.1.call-update) | async-done | bytes 131088 | tf_op jit(solution)/shard_map/psum | solution.py:68
  353.4 1.3 collective-permute-start.3
  354.9 5.4 %collective-permute-done.3 = f32[64,512]{1,0:T(8,128)S(1)} collective-permute-done((f32[64,512]{1,0:T(8,128)S(1)}, f32[64,512]{1,0:T(8,128)S(1)}, u32[]{:S(2)}, u32[]{:S(2)}) %collective-permute-start.3) | collective-permute-done | bytes 131104 | tf_op jit(solution)/shard_map/ppermute | solution.py:12
  360.4 2.7 fusion.15
  363.2 4.4 fusion.5
  367.8 69.6 %all-reduce.19.cloned.1.call-done = f32[64,512]{1,0:T(8,128)} async-done(((f32[64,512]{1,0:T(8,128)}), f32[64,512]{1,0:T(8,128)}) %all-reduce.19.cloned.1.call-update) | async-done | bytes 131088 | tf_op jit(solution)/shard_map/psum | solution.py:68
  (62 shorter events, 20.4 us)
Async XLA Ops:
  6.5 9.5 %copy-start = (bf16[1,64,2048]{2,1,0:T(8,128)(2,1)S(1)}, bf16[1,64,2048]{2,1,0:T(8,128)(2,1)}, u32[]{:S(2)}) copy-start(bf16[1,64,2048]{2,1,0:T(8,128)(2,1)} %param.10) | copy-start | bytes 786436
  6.5 6.1 %copy-start.1 = (bf16[1,64,2048]{2,1,0:T(8,128)(2,1)S(1)}, bf16[1,64,2048]{2,1,0:T(8,128)(2,1)}, u32[]{:S(2)}) copy-start(bf16[1,64,2048]{2,1,0:T(8,128)(2,1)} %param.9) | copy-start | bytes 786436
  6.5 85.8 %all-reduce.11.cloned.1.call-start = ((), (), s32[]{:S(2)}) async-start(), calls=%async_computation | async-start | bytes 262144 | tf_op jit(solution)/shard_map/psum | solution.py:68
  20.5 157.6 %all-reduce.13.cloned.1.call-start = ((), (), s32[]{:S(2)}) async-start(), calls=%async_computation.1 | async-start | bytes 262144 | tf_op jit(solution)/shard_map/psum | solution.py:68
  94.2 6.9 %collective-permute-start = (f32[64,512]{1,0:T(8,128)S(1)}, f32[64,512]{1,0:T(8,128)S(1)}, u32[]{:S(2)}, u32[]{:S(2)}) collective-permute-start(f32[64,512]{1,0:T(8,128)S(1)} %maximum_select_fusion), channel_id=1, source_target_pairs={{0,16},{1,17},{2,18},{3,19},{4,20},{5,21},{6,22},{7,23},{8,24},{9,... | collective-permute-start | bytes 393224 | tf_op jit(solution)/shard_map/ppermute | solution.py:12
  108.4 156.4 %all-reduce.15.cloned.1.call-start = ((), (), s32[]{:S(2)}) async-start(), calls=%async_computation.2 | async-start | bytes 262144 | tf_op jit(solution)/shard_map/psum | solution.py:68
  179.9 7.0 %collective-permute-start.1 = (f32[64,512]{1,0:T(8,128)S(1)}, f32[64,512]{1,0:T(8,128)}, u32[]{:S(2)}, u32[]{:S(2)}) collective-permute-start(f32[64,512]{1,0:T(8,128)S(1)} %maximum_select_fusion.2), channel_id=1, source_target_pairs={{0,16},{1,17},{2,18},{3,19},{4,20},{5,21},{6,22},{7,23},{8,24},{9,... | collective-permute-start | bytes 393224 | tf_op jit(solution)/shard_map/ppermute | solution.py:12
  195.1 156.5 %all-reduce.17.cloned.1.call-start = ((), (), s32[]{:S(2)}) async-start(), calls=%async_computation.3 | async-start | bytes 262144 | tf_op jit(solution)/shard_map/psum | solution.py:68
  266.7 7.0 %collective-permute-start.2 = (f32[64,512]{1,0:T(8,128)S(1)}, f32[64,512]{1,0:T(8,128)}, u32[]{:S(2)}, u32[]{:S(2)}) collective-permute-start(f32[64,512]{1,0:T(8,128)S(1)} %maximum_select_fusion.4), channel_id=1, source_target_pairs={{0,16},{1,17},{2,18},{3,19},{4,20},{5,21},{6,22},{7,23},{8,24},{9,... | collective-permute-start | bytes 393224 | tf_op jit(solution)/shard_map/ppermute | solution.py:12
  281.8 155.5 %all-reduce.19.cloned.1.call-start = ((), (), s32[]{:S(2)}) async-start(), calls=%async_computation.4 | async-start | bytes 262144 | tf_op jit(solution)/shard_map/psum | solution.py:68
  353.4 6.9 %collective-permute-start.3 = (f32[64,512]{1,0:T(8,128)S(1)}, f32[64,512]{1,0:T(8,128)S(1)}, u32[]{:S(2)}, u32[]{:S(2)}) collective-permute-start(f32[64,512]{1,0:T(8,128)S(1)} %maximum_select_fusion.6), channel_id=1, source_target_pairs={{0,16},{1,17},{2,18},{3,19},{4,20},{5,21},{6,22},{7,23},{8,24},{9,... | collective-permute-start | bytes 393224 | tf_op jit(solution)/shard_map/ppermute | solution.py:12
Sparse Core Ops, SparseCore 0:
  20.6 71.6 all-reduce.10
  108.5 69.5 all-reduce.12
  195.2 69.5 all-reduce.14
  281.9 69.5 all-reduce.16
  367.7 69.5 all-reduce.18
where the time goes:
time: 449 us; the launch traced here: 446 us
  waiting for transfers between devices  369 us (82%)
  matrix products  35.7 us (8%)
  between operations  14 us (3%)
  other arithmetic  13.4 us (3%)
  local copies, waits for them, and re-layouts  8.55 us (2%)
  starting transfers between devices  5.33 us (1%)
    psum x5, waiting for transfers between devices, shards(): summed = lax.psum(partial_sum, 'design')  350 us
    dot_general x5, matrix products, local_sum(): lax.dot_general(weight_rows, kernel, (((1,), (1,)), ((), ())), preferred_...  22.1 us
    ppermute x4, waiting for transfers between devices, passed_along(): return lax.ppermute(block, axis, route)  18.7 us
    dot_general x5, matrix products, local_sum(): lax.dot_general(scaled, points, (((0,), (0,)), ((), ())), preferred_eleme...  13.7 us
  transfers between devices with their start and end apart: 9, of which 9 were waited for; matrix products, arithmetic and copies ran while one was open for 1% of the time, Pallas kernels for 0%

commit v1 on v0

v1 whole, which is shorter than its diff:
```python
import functools

import jax
import jax.numpy as jnp
from jax import lax
from jax.experimental import pallas as pl
from jax.experimental.pallas import tpu as pltpu
from jax.sharding import PartitionSpec as P

MICRO = 512
TILE = 256
MESH = pl.DeviceIdType.MESH


def gather_kernel(order_ref, samples_ref, out_ref, rows_ref, picked_ref):
    total = samples_ref.shape[1]
    for start in range(0, total, MICRO):
        rows_ref[start : start + MICRO, :] = samples_ref[:, start : start + MICRO].T
    group = 32

    def pick(step, carry):
        base = pl.multiple_of(step * group, group)
        for k in range(group):
            picked_ref[pl.ds(base + k, 1), :] = rows_ref[pl.ds(order_ref[base + k], 1), :]
        return carry

    lax.fori_loop(0, order_ref.shape[0] // group, pick, 0)
    for turn in range(out_ref.shape[0]):
        out_ref[turn] = picked_ref[turn * MICRO : (turn + 1) * MICRO, :].T


def gather(samples, order):
    feat, total = samples.shape
    return pl.pallas_call(
        gather_kernel,
        out_shape=jax.ShapeDtypeStruct((order.shape[0] // MICRO, feat, MICRO), jnp.float32),
        in_specs=[
            pl.BlockSpec(memory_space=pltpu.SMEM),
            pl.BlockSpec(memory_space=pltpu.VMEM),
        ],
        out_specs=pl.BlockSpec(memory_space=pltpu.VMEM),
        scratch_shapes=[
            pltpu.VMEM((total, feat), jnp.float32),
            pltpu.VMEM((order.shape[0], feat), jnp.float32),
        ],
    )(order, samples)


def softplus(x):
    return jnp.maximum(x, 0.0) + jnp.log1p(jnp.exp(-jnp.abs(x)))


def main_kernel(
    sizes,
    chosen_ref,
    points_ref,
    weights_ref,
    length_ref,
    out_ref,
    sides_ref,
    mean_ref,
    var_ref,
    out_blocks,
    in_blocks,
    land_block,
    land_in,
    sum_sent,
    sum_came,
    land_sent,
    land_came,
):
    devices, count, feat, half, share = sizes
    me = lax.axis_index("design")
    section = lax.axis_index("section")
    is_land = section == 0
    runs = points_ref.shape[2]

    barrier = pltpu.get_barrier_semaphore()

    def greet_peer(step, carry):
        peer = lax.rem(me + step, devices)
        pl.semaphore_signal(barrier, inc=1, device_id={"design": peer}, device_id_type=MESH)
        return carry

    def greet_other(peer, carry):
        pl.semaphore_signal(
            barrier, inc=1, device_id={"section": 1 - section, "design": peer}, device_id_type=MESH
        )
        return carry

    lax.fori_loop(1, devices, greet_peer, 0)
    lax.fori_loop(0, devices, greet_other, 0)

    for start in range(0, runs, MICRO):
        wide = points_ref[0, :, start : start + MICRO].astype(jnp.float32)
        squares = (wide * wide).astype(jnp.bfloat16).astype(jnp.float32)
        both = jnp.concatenate([wide, squares], axis=0)
        sides_ref[start : start + MICRO, :] = both.T.astype(jnp.bfloat16)

    row = jnp.where(is_land, length_ref[0:1, :], length_ref[1:2, :])
    spread = jnp.broadcast_to(row, (feat, feat))
    on_diagonal = lax.broadcasted_iota(jnp.int32, (feat, feat), 0) == lax.broadcasted_iota(
        jnp.int32, (feat, feat), 1
    )
    lengths = jnp.sum(jnp.where(on_diagonal, spread, 0.0), axis=1, keepdims=True)
    var_ref[...] = jnp.zeros_like(var_ref)

    def finish(turn):
        pltpu.make_async_copy(
            in_blocks.at[turn, pl.ds(0, devices - 1)],
            in_blocks.at[turn, pl.ds(0, devices - 1)],
            sum_came.at[turn],
        ).wait()
        total = in_blocks[turn, 0].astype(jnp.float32)
        for peer in range(1, devices):
            total = total + in_blocks[turn, peer].astype(jnp.float32)
        lane = lax.broadcasted_iota(jnp.int32, total.shape, 1)
        total = jnp.where(jnp.logical_and(is_land, lane >= share), softplus(total), total)

        @pl.when(is_land)
        def _():
            land_block[turn] = total

            def pass_on(peer, carry):
                pltpu.make_async_remote_copy(
                    src_ref=land_block.at[turn],
                    dst_ref=land_in.at[turn, me],
                    send_sem=land_sent.at[turn],
                    recv_sem=land_came.at[turn],
                    device_id={"section": 1, "design": peer},
                    device_id_type=MESH,
                ).start()
                return carry

            lax.fori_loop(0, devices, pass_on, 0)

        out_ref[0, turn, :half, :] = total[:, :share]
        out_ref[0, turn, half:, :] = total[:, share:]

    def step(turn, carry):
        @pl.when(is_land)
        def _():
            mean_ref[...] = chosen_ref[turn]

        @pl.when(jnp.logical_not(is_land))
        def _():
            pltpu.make_async_copy(land_in.at[turn], land_in.at[turn], land_came.at[turn]).wait()
            blocks = [land_in[turn, peer] for peer in range(devices)]
            mean_ref[:half, :] = jnp.concatenate([b[:, :share] for b in blocks], axis=1)
            mean_ref[half:, :] = chosen_ref[turn, half:, :]
            var_ref[:half, :] = jnp.concatenate([b[:, share:] for b in blocks], axis=1)

        mean = mean_ref[...]
        var = var_ref[...]
        inverse = 1.0 / (lengths + 2.0 * var)
        scaled = mean * inverse
        bias = -jnp.sum(mean * scaled, axis=0, keepdims=True) - 0.5 * jnp.sum(
            jnp.log(1.0 + 2.0 * var / lengths), axis=0, keepdims=True
        )
        factors = jnp.concatenate(
            [2.0 * scaled.astype(jnp.bfloat16).astype(jnp.float32), -inverse], axis=0
        ).astype(jnp.bfloat16)
        total = jnp.zeros((feat, MICRO), jnp.float32)
        for start in range(0, runs, TILE):
            exponent = jnp.dot(
                sides_ref[start : start + TILE, :], factors, preferred_element_type=jnp.float32
            )
            kernel = jnp.exp(exponent + bias).astype(jnp.bfloat16)
            total = total + jnp.dot(
                weights_ref[0, :, start : start + TILE], kernel, preferred_element_type=jnp.float32
            )
        for peer in range(devices):
            piece = total[:, peer * share : (peer + 1) * share]
            out_blocks[turn, peer] = jnp.concatenate([piece[:half], piece[half:]], axis=1).astype(
                out_blocks.dtype
            )
        in_blocks[turn, me] = out_blocks[turn, me]

        @pl.when(turn == 0)
        def _():
            pl.semaphore_wait(barrier, 2 * devices - 1)

        def hand_over(distance, carry):
            peer = lax.rem(me + distance, devices)
            pltpu.make_async_remote_copy(
                src_ref=out_blocks.at[turn, peer],
                dst_ref=in_blocks.at[turn, me],
                send_sem=sum_sent.at[turn],
                recv_sem=sum_came.at[turn],
                device_id={"design": peer},
                device_id_type=MESH,
            ).start()
            return carry

        lax.fori_loop(1, devices, hand_over, 0)

        @pl.when(turn > 0)
        def _():
            finish(turn - 1)

        return carry

    lax.fori_loop(0, count, step, 0)
    finish(count - 1)

    def drain(turn, carry):
        pltpu.make_async_copy(
            out_blocks.at[turn, pl.ds(0, devices - 1)],
            out_blocks.at[turn, pl.ds(0, devices - 1)],
            sum_sent.at[turn],
        ).wait()

        @pl.when(is_land)
        def _():
            pltpu.make_async_copy(land_in.at[turn], land_in.at[turn], land_sent.at[turn]).wait()

        return carry

    lax.fori_loop(0, count, drain, 0)


def shards(samples, order, design_points, weights, length_sq):
    feat = samples.shape[0]
    runs = design_points.shape[2]
    half = feat // 2
    count = order.shape[0] // MICRO
    devices = lax.axis_size("design")
    share = MICRO // devices
    chosen = gather(samples, order)
    vmem = pl.BlockSpec(memory_space=pltpu.VMEM)
    return pl.pallas_call(
        functools.partial(main_kernel, (devices, count, feat, half, share)),
        out_shape=jax.ShapeDtypeStruct((1, count, feat, share), jnp.float32),
        in_specs=[vmem] * 4,
        out_specs=vmem,
        scratch_shapes=[
            pltpu.VMEM((runs, 2 * feat), jnp.bfloat16),
            pltpu.VMEM((feat, MICRO), jnp.float32),
            pltpu.VMEM((feat, MICRO), jnp.float32),
            pltpu.VMEM((count, devices, half, 2 * share), jnp.bfloat16),
            pltpu.VMEM((count, devices, half, 2 * share), jnp.bfloat16),
            pltpu.VMEM((count, half, 2 * share), jnp.float32),
            pltpu.VMEM((count, devices, half, 2 * share), jnp.float32),
            pltpu.SemaphoreType.DMA((count,)),
            pltpu.SemaphoreType.DMA((count,)),
            pltpu.SemaphoreType.DMA((count,)),
            pltpu.SemaphoreType.DMA((count,)),
        ],
        compiler_params=pltpu.CompilerParams(collective_id=0, has_side_effects=True),
    )(chosen, design_points, weights, length_sq)


def solution(mesh):
    placed = (P(), P("batch"), P("section", None, "design"), P("section", None, "design"), P())
    return jax.shard_map(
        shards,
        mesh=mesh,
        in_specs=placed,
        out_specs=P("section", None, None, ("batch", "design")),
        check_vma=False,
    )
```

time: 449 us -> 41.1 us (0.09)
  waiting for transfers between devices: 369 us -> 0 us
  Pallas kernels: 0 us -> 39.3 us
  matrix products: 35.7 us -> 0 us
  between operations: 14 us -> 0.01 us
  other arithmetic: 13.4 us -> 0 us
  local copies, waits for them, and re-layouts: 8.55 us -> 1.57 us
  starting transfers between devices: 5.33 us -> 0 us
    psum x5 -> x0, waiting for transfers between devices: 350 us -> none  [shards(): summed = lax.psum(partial_sum, 'design')]
    pallas_call x0 -> x2, Pallas kernels: none -> 39.3 us  [the longest x1 34.4 us: shards(): pl.pallas_call(functools.partial(main_kernel, (devices, count, feat, half...]
    dot_general x10 -> x0, matrix products: 35.7 us -> none  [the longest x5 22.1 us: local_sum(): lax.dot_general(weight_rows, kernel, (((1,), (1,)), ((), ())), preferred_...]
    ppermute x4 -> x0, waiting for transfers between devices: 18.7 us -> none  [passed_along(): return lax.ppermute(block, axis, route)]
    select_n x8 -> x0, other arithmetic: 6.11 us -> none  [the longest x4 3.74 us: shards(): jnp.where(is_first, jnp.concatenate([summed[:half], jax.nn.softplus(summe...]
    ppermute x4 -> x0, starting transfers between devices: 5.17 us -> none  [passed_along(): return lax.ppermute(block, axis, route)]
    gather x8 -> x0, local copies, waits for them, and re-layouts: 4.6 us -> none  [pick(): return jnp.take(samples, indices, axis=1)]
  transfers between devices with their start and end apart: 9 -> 0, of which waited for: 9 -> 0; matrix products, arithmetic and copies ran while one was open for 1% -> 0% of each run, Pallas kernels for 0% -> 0%
where the time goes in v1:
time: 41.1 us; the launch traced here: 40.9 us
  Pallas kernels  39.3 us (96%)
  local copies, waits for them, and re-layouts  1.57 us (4%)
    pallas_call x1, Pallas kernels, shards(): pl.pallas_call(functools.partial(main_kernel, (devices, count, feat, half...  34.4 us
    pallas_call x1, Pallas kernels, gather(): pl.pallas_call(gather_kernel, out_shape=jax.ShapeDtypeStruct((order.shape...  4.86 us
    unnamed x1, local copies, waits for them, and re-layouts  1.57 us

profile of v1, /device:TPU:4, one launch (start us, length us, event | category | flops | bytes accessed | tf_op | source)
XLA Modules:
  0.0 40.9 jit_solution(9305907459932529591)
XLA Ops:
  0.0 4.9 %shard_map.55.chosen_ref = f32[4,64,512]{2,1,0:T(8,128)} custom-call(s32[2048]{0:T(1024)} %order_ref.1, f32[64,4096]{1,0:T(8,128)} %samples_ref.1), custom_call_target="tpu_custom_call" | custom-call | tf_op jit(solution)/shard_map/pallas_call | solution.py:34
  4.9 34.4 %shard_map.56 = f32[1,4,64,64]{3,2,1,0:T(8,128)} custom-call(f32[4,64,512]{2,1,0:T(8,128)} %shard_map.55.chosen_ref, bf16[1,64,2048]{2,1,0:T(8,128)(2,1)} %points_ref.1, bf16[1,64,2048]{2,1,0:T(8,128)(2,1)} %weights_ref.1, f32[2,64]{1,0:T(2,128)} %length_ref.1), custom_call_target="tpu_custom_call" | custom-call | tf_op jit(solution)/shard_map/pallas_call | solution.py:231
  39.3 1.6 %copy.7 = f32[1,4,64,64]{3,2,1,0:T(8,128)} copy(f32[1,4,64,64]{3,2,1,0:T(8,128)} %shard_map.56) | data formatting | bytes 131072

commit v2 on v1

--- a/solution.py
+++ b/solution.py
@@ -12,51 +12,20 @@
 MESH = pl.DeviceIdType.MESH
 
 
-def gather_kernel(order_ref, samples_ref, out_ref, rows_ref, picked_ref):
-    total = samples_ref.shape[1]
-    for start in range(0, total, MICRO):
-        rows_ref[start : start + MICRO, :] = samples_ref[:, start : start + MICRO].T
-    group = 32
-
-    def pick(step, carry):
-        base = pl.multiple_of(step * group, group)
-        for k in range(group):
-            picked_ref[pl.ds(base + k, 1), :] = rows_ref[pl.ds(order_ref[base + k], 1), :]
-        return carry
-
-    lax.fori_loop(0, order_ref.shape[0] // group, pick, 0)
-    for turn in range(out_ref.shape[0]):
-        out_ref[turn] = picked_ref[turn * MICRO : (turn + 1) * MICRO, :].T
-
-
-def gather(samples, order):
-    feat, total = samples.shape
-    return pl.pallas_call(
-        gather_kernel,
-        out_shape=jax.ShapeDtypeStruct((order.shape[0] // MICRO, feat, MICRO), jnp.float32),
-        in_specs=[
-            pl.BlockSpec(memory_space=pltpu.SMEM),
-            pl.BlockSpec(memory_space=pltpu.VMEM),
-        ],
-        out_specs=pl.BlockSpec(memory_space=pltpu.VMEM),
-        scratch_shapes=[
-            pltpu.VMEM((total, feat), jnp.float32),
-            pltpu.VMEM((order.shape[0], feat), jnp.float32),
-        ],
-    )(order, samples)
-
-
 def softplus(x):
     return jnp.maximum(x, 0.0) + jnp.log1p(jnp.exp(-jnp.abs(x)))
 
 
 def main_kernel(
     sizes,
-    chosen_ref,
+    order_ref,
+    samples_ref,
     points_ref,
     weights_ref,
     length_ref,
     out_ref,
+    rows_ref,
+    picked_ref,
     sides_ref,
     mean_ref,
     var_ref,
@@ -91,6 +60,16 @@
     lax.fori_loop(1, devices, greet_peer, 0)
     lax.fori_loop(0, devices, greet_other, 0)
 
+    for start in range(0, samples_ref.shape[1], MICRO):
+        rows_ref[start : start + MICRO, :] = samples_ref[:, start : start + MICRO].T
+
+    def pick(source, slot, first, number):
+        for at in range(first, first + number):
+            index = order_ref[source * MICRO + at]
+            picked_ref[slot, at : at + 1, :] = rows_ref[pl.ds(index, 1), :]
+
+    pick(0, 0, 0, MICRO)
+
     for start in range(0, runs, MICRO):
         wide = points_ref[0, :, start : start + MICRO].astype(jnp.float32)
         squares = (wide * wide).astype(jnp.bfloat16).astype(jnp.float32)
@@ -138,16 +117,19 @@
         out_ref[0, turn, half:, :] = total[:, share:]
 
     def step(turn, carry):
+        slot = lax.rem(turn, 2)
+        chosen = picked_ref[slot].T
+
         @pl.when(is_land)
         def _():
-            mean_ref[...] = chosen_ref[turn]
+            mean_ref[...] = chosen
 
         @pl.when(jnp.logical_not(is_land))
         def _():
             pltpu.make_async_copy(land_in.at[turn], land_in.at[turn], land_came.at[turn]).wait()
             blocks = [land_in[turn, peer] for peer in range(devices)]
             mean_ref[:half, :] = jnp.concatenate([b[:, :share] for b in blocks], axis=1)
-            mean_ref[half:, :] = chosen_ref[turn, half:, :]
+            mean_ref[half:, :] = chosen[half:, :]
             var_ref[:half, :] = jnp.concatenate([b[:, share:] for b in blocks], axis=1)
 
         mean = mean_ref[...]
@@ -161,7 +143,10 @@
             [2.0 * scaled.astype(jnp.bfloat16).astype(jnp.float32), -inverse], axis=0
         ).astype(jnp.bfloat16)
         total = jnp.zeros((feat, MICRO), jnp.float32)
+        following = jnp.minimum(turn + 1, count - 1)
+        portion = MICRO * TILE // runs
         for start in range(0, runs, TILE):
+            pick(following, 1 - slot, start // TILE * portion, portion)
             exponent = jnp.dot(
                 sides_ref[start : start + TILE, :], factors, preferred_element_type=jnp.float32
             )
@@ -226,14 +211,15 @@
     count = order.shape[0] // MICRO
     devices = lax.axis_size("design")
     share = MICRO // devices
-    chosen = gather(samples, order)
     vmem = pl.BlockSpec(memory_space=pltpu.VMEM)
     return pl.pallas_call(
         functools.partial(main_kernel, (devices, count, feat, half, share)),
         out_shape=jax.ShapeDtypeStruct((1, count, feat, share), jnp.float32),
-        in_specs=[vmem] * 4,
+        in_specs=[pl.BlockSpec(memory_space=pltpu.SMEM)] + [vmem] * 4,
         out_specs=vmem,
         scratch_shapes=[
+            pltpu.VMEM((samples.shape[1], feat), jnp.float32),
+            pltpu.VMEM((2, MICRO, feat), jnp.float32),
             pltpu.VMEM((runs, 2 * feat), jnp.bfloat16),
             pltpu.VMEM((feat, MICRO), jnp.float32),
             pltpu.VMEM((feat, MICRO), jnp.float32),
@@ -247,7 +233,7 @@
             pltpu.SemaphoreType.DMA((count,)),
         ],
         compiler_params=pltpu.CompilerParams(collective_id=0, has_side_effects=True),
-    )(chosen, design_points, weights, length_sq)
+    )(order, samples, design_points, weights, length_sq)
 
 
 def solution(mesh):

time: 41.1 us -> 36.1 us (0.88)
  Pallas kernels: 39.3 us -> 34.4 us
    pallas_call x1 -> x0, Pallas kernels: 4.86 us -> none  [gather(): pl.pallas_call(gather_kernel, out_shape=jax.ShapeDtypeStruct((order.shape...]
where the time goes in v2:
time: 36.1 us; the launch traced here: 35.9 us
  Pallas kernels  34.4 us (95%)
  local copies, waits for them, and re-layouts  1.57 us (4%)
    pallas_call x1, Pallas kernels, shards(): pl.pallas_call(functools.partial(main_kernel, (devices, count, feat, half...  34.4 us
    unnamed x1, local copies, waits for them, and re-layouts  1.57 us

profile of v2, /device:TPU:4, one launch (start us, length us, event | category | flops | bytes accessed | tf_op | source)
XLA Modules:
  0.0 35.9 jit_solution(9563491386704175835)
XLA Ops:
  0.0 34.4 %shard_map.55 = f32[1,4,64,64]{3,2,1,0:T(8,128)} custom-call(s32[2048]{0:T(1024)} %order_ref.1, f32[64,4096]{1,0:T(8,128)} %samples_ref.1, bf16[1,64,2048]{2,1,0:T(8,128)(2,1)} %points_ref.1, bf16[1,64,2048]{2,1,0:T(8,128)(2,1)} %weights_ref.1, f32[2,64]{1,0:T(2,128)} %length_ref.1), custom_call_target="tpu_custom_call" | custom-call | tf_op jit(solution)/shard_map/pallas_call | solution.py:215
  34.4 1.6 %copy.7 = f32[1,4,64,64]{3,2,1,0:T(8,128)} copy(f32[1,4,64,64]{3,2,1,0:T(8,128)} %shard_map.55) | data formatting | bytes 131072
